TPU v7x, 32 devices: a whole 2x2x4 slice. The times are simulated.
32 devices in a mesh: ctx: 4 (over z), head: 4 (over y, x), fsdp: 2 (over core).
Axes of the slice: x: 2, y: 2, z: 4, core: 2. Of those that a mesh axis runs over, the one named last changes fastest.
Arguments:
- query_rows: bfloat16 [4096, 6144], P(('ctx', 'head'), 'fsdp'), may hold values from -400 to 400
- key_rows: bfloat16 [4096, 6144], P(('ctx', 'head'), 'fsdp'), may hold values from -8 to 8
- value_rows: bfloat16 [4096, 4096], P(('ctx', 'head'), 'fsdp'), may hold values from -6 to 6
- query_weight: bfloat16 [1536, 6144], P(('ctx', 'fsdp'), 'head'), may hold values from -6 to 6
- key_weight: bfloat16 [512, 4096], P(('ctx', 'fsdp'), 'head'), may hold values from -6 to 6
Outputs:
- attended: bfloat16 [4096, 4096], P('ctx', ('fsdp', 'head'))
- clipped_query: bfloat16 [1536, 6144], P(('ctx', 'fsdp'), 'head')
- clipped_key: bfloat16 [512, 4096], P(('ctx', 'fsdp'), 'head')
All inputs are finite; a program needn't handle non-finite values.
Results may differ from a plain program's by a relative error of at most 0.0033.
Values may be sent and summed in bfloat16 or wider, within the bound.
No kernel may reach another device: no remote copies, remote signals or barrier semaphores. Data moves between devices by JAX's collectives and lax.ppermute only.
A program may use at most 128 MiB of HBM per device.

v0:
```python
import jax
import jax.numpy as jnp
from jax import lax
from jax.sharding import PartitionSpec as P

DNOPE = 128
DROPE = 64
DV = 128
DQK = 192


clip_threshold = 100.0


def shifted_2(value, axis, steps):
    count = lax.axis_size(axis)
    first, last = (max(0, -steps), min(count, count - steps))
    return lax.ppermute(value, axis, [(source, source + steps) for source in range(first, last)])


def partial_softmax(scores, value_cube):
    highest = jnp.max(scores, axis=2)
    present = jnp.isfinite(highest)
    shifted = jnp.where(present, highest, 0.0)
    weights = jnp.exp(scores - shifted[:, :, None])
    totals = jnp.sum(weights, axis=2)
    rounded = weights.astype(jnp.bfloat16)
    summed = jnp.einsum("htu,uhd->thd", rounded, value_cube, preferred_element_type=jnp.float32)
    return (summed, totals, jnp.where(present, highest, -jnp.inf))


def merge_parts(own_part, far_part):
    own_sum, own_total, own_high = own_part
    far_sum, far_total, far_high = far_part
    highest = jnp.maximum(own_high, far_high)
    own_scale = jnp.exp(own_high - highest)
    far_scale = jnp.exp(far_high - highest)
    totals = own_total * own_scale + far_total * far_scale
    mixed = own_sum * own_scale.T[:, :, None] + far_sum * far_scale.T[:, :, None]
    return mixed / totals.T[:, :, None]


def head_scores(query_cube, key_cube):
    return jnp.einsum(
        "thd,uhd->htu", query_cube, key_cube, preferred_element_type=jnp.float32
    ) * DQK ** (-0.5)


def causal_block(query_cube, key_cube, value_cube, row_start, block_rows):
    row_count = key_cube.shape[0]
    query_block = query_cube[row_start : row_start + block_rows]
    row_ids = lax.broadcasted_iota(jnp.int32, (block_rows, row_count), 0) + row_start
    col_ids = lax.broadcasted_iota(jnp.int32, (block_rows, row_count), 1)
    scores = jnp.where((row_ids >= col_ids)[None], head_scores(query_block, key_cube), -jnp.inf)
    return (partial_softmax(scores, value_cube), jnp.max(scores, axis=(1, 2)))


def body(query_rows, key_rows, value_rows, query_weight, key_weight):
    local_query, local_key, local_value = (
        lax.all_to_all(query_rows, "head", split_axis=1, concat_axis=0, tiled=True),
        lax.all_to_all(key_rows, "head", split_axis=1, concat_axis=0, tiled=True),
        lax.all_to_all(value_rows, "head", split_axis=1, concat_axis=0, tiled=True),
    )
    row_count = local_query.shape[0]
    head_count = local_query.shape[1] // DQK
    query_cube = local_query.reshape(row_count, head_count, DQK)
    key_cube = local_key.reshape(row_count, head_count, DQK)
    value_cube = local_value.reshape(row_count, head_count, DV)
    block_index = lax.axis_index("ctx")
    block_rows = min(512, row_count)
    row_starts = list(range(0, row_count, block_rows))
    local_peak = jnp.full((head_count,), -jnp.inf, jnp.float32)
    pieces = []
    far_key, far_value = shifted_2((local_key, local_value), "ctx", 1)
    far_keys = far_key.reshape(row_count, head_count, DQK)
    far_values = far_value.reshape(row_count, head_count, DV)
    for row_start in row_starts:
        own_part, own_peak = causal_block(query_cube, key_cube, value_cube, row_start, block_rows)
        far_scores = jnp.where(
            block_index > 0,
            head_scores(query_cube[row_start : row_start + block_rows], far_keys),
            -jnp.inf,
        )
        far_part = partial_softmax(far_scores, far_values)
        local_peak = jnp.maximum(
            local_peak, jnp.maximum(own_peak, jnp.max(far_scores, axis=(1, 2)))
        )
        pieces.append(merge_parts(own_part, far_part))
    attended = (
        jnp.concatenate(pieces, axis=0).astype(jnp.bfloat16).reshape(row_count, head_count * DV)
    )
    weight_heads = key_weight.shape[1] // DNOPE
    cycle_peak = lax.pmax(local_peak, "ctx")
    gathered = lax.all_gather(cycle_peak, ("head", "fsdp"), axis=0, tiled=True)
    head_peak = (
        gathered.reshape(lax.axis_size("head"), lax.axis_size("fsdp"), head_count)
        .transpose(1, 0, 2)
        .reshape(-1)
    )
    own_peaks = lax.dynamic_slice_in_dim(
        head_peak, lax.axis_index("head") * weight_heads, weight_heads, 0
    )
    factor = jnp.minimum(1.0, clip_threshold / own_peaks)
    root_factor = jnp.sqrt(factor)
    column_factor = jnp.concatenate(
        [
            jnp.broadcast_to(root_factor[:, None], (weight_heads, DNOPE)),
            jnp.broadcast_to(factor[:, None], (weight_heads, DROPE)),
        ],
        axis=1,
    )
    query_count = query_weight.shape[0]
    key_count = key_weight.shape[0]
    clipped_query = (
        (
            query_weight.astype(jnp.float32).reshape(query_count, weight_heads, DQK)
            * column_factor[None]
        )
        .astype(jnp.bfloat16)
        .reshape(query_count, weight_heads * DQK)
    )
    clipped_key = (
        (
            key_weight.astype(jnp.float32).reshape(key_count, weight_heads, DNOPE)
            * root_factor[None, :, None]
        )
        .astype(jnp.bfloat16)
        .reshape(key_count, weight_heads * DNOPE)
    )
    return (attended, clipped_query, clipped_key)


def solution(mesh):
    return jax.shard_map(
        body,
        mesh=mesh,
        in_specs=(
            P(("ctx", "head"), "fsdp"),
            P(("ctx", "head"), "fsdp"),
            P(("ctx", "head"), "fsdp"),
            P(("ctx", "fsdp"), "head"),
            P(("ctx", "fsdp"), "head"),
        ),
        out_specs=(
            P("ctx", ("fsdp", "head")),
            P(("ctx", "fsdp"), "head"),
            P(("ctx", "fsdp"), "head"),
        ),
        check_vma=False,
    )
```

profile of v0, /device:TPU:0, one launch (start us, length us, event | category | flops | bytes accessed | tf_op | source)
XLA Modules:
  0.0 180.5 jit_solution(10534738147140960069)
XLA Ops:
  0.6 2.3 %copy.29 = bf16[256,2048]{0,1:T(8,128)(2,1)} copy(bf16[256,2048]{1,0:T(8,128)(2,1)} %param.7) | data formatting | bytes 2097152 | tf_op args[2]
  2.9 5.2 %all-to-all-start.2 = ((bf16[256,4,512]{0,2,1:T(8,128)(2,1)}), bf16[256,4,512]{0,2,1:T(8,128)(2,1)S(1)}, u32[]{:S(2)}, u32[]{:S(2)}) async-start(bf16[256,4,512]{0,2,1:T(8,128)(2,1)} %bitcast.5), calls=%async_computation.2 | async-start | bytes 2097152 | tf_op jit(solution)/shard_map/all_to_all | solution.py:62
  8.1 2.6 %copy.26 = bf16[256,3072]{0,1:T(8,128)(2,1)} copy(bf16[256,3072]{1,0:T(8,128)(2,1)} %param.6) | data formatting | bytes 3145728 | tf_op args[1]
  10.7 11.0 %all-to-all-done.2 = bf16[256,4,512]{0,2,1:T(8,128)(2,1)S(1)} async-done(((bf16[256,4,512]{0,2,1:T(8,128)(2,1)}), bf16[256,4,512]{0,2,1:T(8,128)(2,1)S(1)}, u32[]{:S(2)}, u32[]{:S(2)}) %all-to-all-start.2) | async-done | bytes 1048608 | tf_op jit(solution)/shard_map/all_to_all | solution.py:62
  21.7 3.6 %all-to-all-start.1 = ((bf16[256,4,768]{0,2,1:T(8,128)(2,1)}), bf16[256,4,768]{0,2,1:T(8,128)(2,1)S(1)}, u32[]{:S(2)}, u32[]{:S(2)}) async-start(bf16[256,4,768]{0,2,1:T(8,128)(2,1)} %bitcast.115), calls=%async_computation.1 | async-start | bytes 3145728 | tf_op jit(solution)/shard_map/all_to_all | solution.py:61
  25.3 2.6 %copy.24 = bf16[256,3072]{0,1:T(8,128)(2,1)} copy(bf16[256,3072]{1,0:T(8,128)(2,1)} %param.5) | data formatting | bytes 3145728 | tf_op args[0]
  27.9 16.1 %all-to-all-done.1 = bf16[256,4,768]{0,2,1:T(8,128)(2,1)S(1)} async-done(((bf16[256,4,768]{0,2,1:T(8,128)(2,1)}), bf16[256,4,768]{0,2,1:T(8,128)(2,1)S(1)}, u32[]{:S(2)}, u32[]{:S(2)}) %all-to-all-start.1) | async-done | bytes 1572896 | tf_op jit(solution)/shard_map/all_to_all | solution.py:61
  44.0 4.3 %all-to-all-start = ((bf16[256,4,768]{0,2,1:T(8,128)(2,1)}), bf16[256,4,768]{0,2,1:T(8,128)(2,1)}, u32[]{:S(2)}, u32[]{:S(2)}) async-start(bf16[256,4,768]{0,2,1:T(8,128)(2,1)} %bitcast.114), calls=%async_computation | async-start | bytes 3145728 | tf_op jit(solution)/shard_map/all_to_all | solution.py:60
  51.8 1.8 copy.31
  53.6 2.6 %reshape.100 = bf16[1024,4,128]{0,2,1:T(8,128)(2,1)} reshape(bf16[4,256,512]{1,0,2:T(4,128)(2,1)} %copy.31) | data formatting | bytes 2097152 | tf_op jit(solution)/shard_map/reshape | solution.py:68
  57.4 4.5 %collective-permute-start.1 = (bf16[1024,512]{1,0:T(8,128)(2,1)}, bf16[1024,512]{1,0:T(8,128)(2,1)}, u32[]{:S(2)}, u32[]{:S(2)}) collective-permute-start(bf16[1024,512]{1,0:T(8,128)(2,1)} %bitcast.118), channel_id=1, source_target_pairs={{0,8},{8,16},{16,24},{1,9},{9,17},{17,25},{2,10},{10,18},{18,26},{... | collective-permute-start | bytes 3145736 | tf_op jit(solution)/shard_map/ppermute | solution.py:18
  62.0 1.6 copy.27
  63.6 3.6 %collective-permute-start = (bf16[1024,768]{1,0:T(8,128)(2,1)}, bf16[1024,768]{1,0:T(8,128)(2,1)}, u32[]{:S(2)}, u32[]{:S(2)}) collective-permute-start(bf16[1024,768]{1,0:T(8,128)(2,1)} %bitcast.10), channel_id=1, source_target_pairs={{0,8},{8,16},{16,24},{1,9},{9,17},{17,25},{2,10},{10,18},{18,26},{... | collective-permute-start | bytes 4718600 | tf_op jit(solution)/shard_map/ppermute | solution.py:18
  67.2 1.5 fusion.81
  69.5 1.4 slice.17
  71.7 1.4 slice.15
  74.3 2.5 %reshape.99 = bf16[1024,4,192]{0,2,1:T(8,128)(2,1)} reshape(bf16[4,256,768]{1,0,2:T(4,128)(2,1)S(1)} %copy.28) | data formatting | bytes 3145728 | tf_op jit(solution)/shard_map/reshape | solution.py:67
  76.8 3.8 %fusion.13 = (f32[4,512]{1,0:T(4,128)S(1)}, f32[4,512,1024]{2,1,0:T(8,128)S(1)}) fusion(pred[512,1024]{1,0:T(8,128)(4,1)} %iota_compare_fusion, bf16[512,4,192]{0,2,1:T(8,128)(2,1)} %slice.17, bf16[1024,4,192]{0,2,1:T(8,128)(2,1)} %reshape.99), kind=kOutput, calls=%fused_computation.21 | convolution fusion | flops 811595776 | bytes 11280384 | tf_op jit(solution)/shard_map/thd,uhd->htu/dot_general | solution.py:44
  80.7 1.9 %fusion.9 = (f32[4,512]{1,0:T(4,128)S(1)}, f32[4,512,1024]{2,1,0:T(8,128)S(1)}) fusion(pred[512,1024]{1,0:T(8,128)(4,1)S(1)} %copy-done.5, bf16[512,4,192]{0,2,1:T(8,128)(2,1)S(1)} %copy-done.9, bf16[1024,4,192]{0,2,1:T(8,128)(2,1)S(1)} %copy-done.6), kind=kOutput, calls=%fused_computation.17 | convolution fusion | flops 811595776 | bytes 11280384 | tf_op jit(solution)/shard_map/thd,uhd->htu/dot_general | solution.py:44
  82.7 5.6 %fusion.8 = (f32[4]{0:T(128)S(1)}, f32[4,512]{1,0:T(4,128)S(1)}, f32[4,512]{1,0:T(4,128)S(1)}, f32[4]{0:T(128)S(1)}) fusion(f32[4,512,1024]{2,1,0:T(8,128)S(1)} %get-tuple-element.26, pred[512,1024]{1,0:T(8,128)(4,1)S(1)} %copy-done.5, f32[4,512]{1,0:T(4,128)S(1)} %is-finite_select_fusion.7, f32[4,512]{1,0:T(4,128)S(1)} %is-finite_select_fusion.3, ...), kind=kLoop, calls=%fused_computation.16 | loop fusion | flops 20967416 | bytes 17858592 | tf_op jit(solution)/shard_map/reduce_max | solution.py:55
  88.3 28.4 %collective-permute-done = bf16[1024,768]{1,0:T(8,128)(2,1)} collective-permute-done((bf16[1024,768]{1,0:T(8,128)(2,1)}, bf16[1024,768]{1,0:T(8,128)(2,1)}, u32[]{:S(2)}, u32[]{:S(2)}) %collective-permute-start) | collective-permute-done | bytes 1572896 | tf_op jit(solution)/shard_map/ppermute | solution.py:18
  116.6 1.7 copy.32
  118.4 1.5 fusion.15
  119.9 1.5 fusion.11
  121.5 4.6 %fusion.10 = (f32[4]{0:T(128)S(1)}, f32[4,512]{1,0:T(4,128)S(1)}, f32[4,512]{1,0:T(4,128)S(1)}, f32[4]{0:T(128)S(1)}) fusion(f32[4,512,1024]{2,1,0:T(8,128)S(1)} %get-tuple-element.28, pred[]{:T(512)S(6)} %gt.4, f32[4,512]{1,0:T(4,128)S(1)} %is-finite_select_fusion.4, f32[4,512]{1,0:T(4,128)S(1)} %is-finite_select_fusion, ...), kind=kLoop, calls=%fused_computation.18 | loop fusion | flops 20967416 | bytes 16810016 | tf_op jit(solution)/shard_map/reduce_max | solution.py:86
  126.1 1.5 copy.33
  127.6 12.9 %pmax.7 = f32[4]{0:T(128)S(1)} all-reduce(f32[4]{0:T(128)S(1)} %maximum_maximum_fusion), channel_id=1, replica_groups=mesh['ctx'=4,'head'=4,'fsdp'=2] {'ctx'}, use_global_device_ids=true, to_apply=%region_12.13 | all-reduce | flops 4 | bytes 32 | tf_op jit(solution)/shard_map/pmax | solution.py:93
  140.8 12.0 %all-reduce.1 = f32[32]{0:T(128)S(1)} all-reduce(f32[32]{0:T(128)S(1)} %reshape.104), channel_id=1, replica_groups=mesh['ctx'=4,'head'=4,'fsdp'=2] {'head','fsdp'}, use_global_device_ids=true, to_apply=%add | all-reduce | flops 32 | bytes 256
  153.3 4.7 %fusion.49 = f32[512,4,128]{0,2,1:T(8,128)S(1)} fusion(bf16[1024,4,128]{0,2,1:T(8,128)(2,1)S(1)} %copy-done.7, f32[4,512,1024]{2,1,0:T(8,128)} %copy-done.3, f32[4,512]{1,0:T(4,128)S(1)} %is-finite_select_fusion.7, pred[512,1024]{1,0:T(8,128)(4,1)S(1)} %copy-done.5, f32[512,4]{0,1:T(4,128)S(1)} %get-tuple-element.15), kind=kOutput, calls=%fused_computation.41 | convolution fusion | flops 545521664 | bytes 11026432 | tf_op jit(solution)/shard_map/htu,uhd->thd/dot_general | solution.py:28
  158.0 6.3 %divide_convert_fusion.1 = bf16[512,4,128]{0,2,1:T(8,128)(2,1)} fusion(f32[512,4,128]{0,2,1:T(8,128)S(1)} %fusion.49, bf16[1024,4,128]{0,2,1:T(8,128)(2,1)S(1)} %bitcast.119, f32[4,512,1024]{2,1,0:T(8,128)} %copy-done.1, f32[4,512]{1,0:T(4,128)S(1)} %is-finite_select_fusion.4, pred[]{:T(512)S(6)} %gt.4, f32[512,4]{0,1:T(4,128)S(1)} %get-tuple-element.13, ...), kind=kOutput, calls=%fused_computation.47 | convolution fusion | flops 546308096 | bytes 11034625 | tf_op jit(solution)/shard_map/htu,uhd->thd/dot_general | solution.py:28
  165.5 4.7 %fusion.46 = f32[512,4,128]{0,2,1:T(8,128)S(1)} fusion(bf16[1024,4,128]{0,2,1:T(8,128)(2,1)S(1)} %copy-done.7, f32[4,512,1024]{2,1,0:T(8,128)} %copy-done.2, f32[4,512]{1,0:T(4,128)S(1)} %is-finite_select_fusion.3, pred[512,1024]{1,0:T(8,128)(4,1)S(1)} %copy-done.4, f32[512,4]{0,1:T(4,128)S(1)} %get-tuple-element.18), kind=kOutput, calls=%fused_computation.40 | convolution fusion | flops 545521664 | bytes 11026432 | tf_op jit(solution)/shard_map/htu,uhd->thd/dot_general | solution.py:28
  170.2 6.3 %divide_convert_fusion = bf16[512,4,128]{0,2,1:T(8,128)(2,1)} fusion(f32[512,4,128]{0,2,1:T(8,128)S(1)} %fusion.46, bf16[1024,4,128]{0,2,1:T(8,128)(2,1)S(1)} %bitcast.120, f32[4,512,1024]{2,1,0:T(8,128)} %copy-done, f32[4,512]{1,0:T(4,128)S(1)} %is-finite_select_fusion, pred[]{:T(512)S(6)} %gt.4, f32[512,4]{0,1:T(4,128)S(1)} %get-tuple-element.16, ...), kind=kOutput, calls=%fused_computation.46 | convolution fusion | flops 546308096 | bytes 11034625 | tf_op jit(solution)/shard_map/htu,uhd->thd/dot_general | solution.py:28
  (61 shorter events, 12.9 us)
Async XLA Ops:
  0.6 47.8 %copy-start.13 = (u32[32]{0:T(128)S(1)}, u32[32]{0:T(128)}, u32[]{:S(2)}) copy-start(u32[32]{0:T(128)} %constant.30) | copy-start | bytes 388
  2.9 18.8 %all-to-all-start.2 = ((bf16[256,4,512]{0,2,1:T(8,128)(2,1)}), bf16[256,4,512]{0,2,1:T(8,128)(2,1)S(1)}, u32[]{:S(2)}, u32[]{:S(2)}) async-start(bf16[256,4,512]{0,2,1:T(8,128)(2,1)} %bitcast.5), calls=%async_computation.2 | async-start | bytes 2097152 | tf_op jit(solution)/shard_map/all_to_all | solution.py:62
  21.7 22.3 %all-to-all-start.1 = ((bf16[256,4,768]{0,2,1:T(8,128)(2,1)}), bf16[256,4,768]{0,2,1:T(8,128)(2,1)S(1)}, u32[]{:S(2)}, u32[]{:S(2)}) async-start(bf16[256,4,768]{0,2,1:T(8,128)(2,1)} %bitcast.115), calls=%async_computation.1 | async-start | bytes 3145728 | tf_op jit(solution)/shard_map/all_to_all | solution.py:61
  44.0 23.2 %all-to-all-start = ((bf16[256,4,768]{0,2,1:T(8,128)(2,1)}), bf16[256,4,768]{0,2,1:T(8,128)(2,1)}, u32[]{:S(2)}, u32[]{:S(2)}) async-start(bf16[256,4,768]{0,2,1:T(8,128)(2,1)} %bitcast.114), calls=%async_computation | async-start | bytes 3145728 | tf_op jit(solution)/shard_map/all_to_all | solution.py:60
  57.4 68.6 %collective-permute-start.1 = (bf16[1024,512]{1,0:T(8,128)(2,1)}, bf16[1024,512]{1,0:T(8,128)(2,1)}, u32[]{:S(2)}, u32[]{:S(2)}) collective-permute-start(bf16[1024,512]{1,0:T(8,128)(2,1)} %bitcast.118), channel_id=1, source_target_pairs={{0,8},{8,16},{16,24},{1,9},{9,17},{17,25},{2,10},{10,18},{18,26},{... | collective-permute-start | bytes 3145736 | tf_op jit(solution)/shard_map/ppermute | solution.py:18
  63.6 53.1 %collective-permute-start = (bf16[1024,768]{1,0:T(8,128)(2,1)}, bf16[1024,768]{1,0:T(8,128)(2,1)}, u32[]{:S(2)}, u32[]{:S(2)}) collective-permute-start(bf16[1024,768]{1,0:T(8,128)(2,1)} %bitcast.10), channel_id=1, source_target_pairs={{0,8},{8,16},{16,24},{1,9},{9,17},{17,25},{2,10},{10,18},{18,26},{... | collective-permute-start | bytes 4718600 | tf_op jit(solution)/shard_map/ppermute | solution.py:18
  74.3 6.3 %copy-start.5 = (pred[512,1024]{1,0:T(8,128)(4,1)S(1)}, pred[512,1024]{1,0:T(8,128)(4,1)}, u32[]{:S(2)}) copy-start(pred[512,1024]{1,0:T(8,128)(4,1)} %iota_compare_fusion.1) | copy-start | bytes 1572868
  76.8 3.8 %copy-start.6 = (bf16[1024,4,192]{0,2,1:T(8,128)(2,1)S(1)}, bf16[1024,4,192]{0,2,1:T(8,128)(2,1)}, u32[]{:S(2)}) copy-start(bf16[1024,4,192]{0,2,1:T(8,128)(2,1)} %reshape.99) | copy-start | bytes 4718596
  76.8 3.8 %copy-start.9 = (bf16[512,4,192]{0,2,1:T(8,128)(2,1)S(1)}, bf16[512,4,192]{0,2,1:T(8,128)(2,1)}, u32[]{:S(2)}) copy-start(bf16[512,4,192]{0,2,1:T(8,128)(2,1)} %slice.15) | copy-start | bytes 2359300
  80.7 7.6 %copy-start.2 = (f32[4,512,1024]{2,1,0:T(8,128)}, f32[4,512,1024]{2,1,0:T(8,128)S(1)}, u32[]{:S(2)}) copy-start(f32[4,512,1024]{2,1,0:T(8,128)S(1)} %get-tuple-element.22) | copy-start | bytes 25165828
  80.7 2.0 %copy-start.4 = (pred[512,1024]{1,0:T(8,128)(4,1)S(1)}, pred[512,1024]{1,0:T(8,128)(4,1)}, u32[]{:S(2)}) copy-start(pred[512,1024]{1,0:T(8,128)(4,1)} %iota_compare_fusion) | copy-start | bytes 1572868
  82.6 5.7 %copy-start.3 = (f32[4,512,1024]{2,1,0:T(8,128)}, f32[4,512,1024]{2,1,0:T(8,128)S(1)}, u32[]{:S(2)}) copy-start(f32[4,512,1024]{2,1,0:T(8,128)S(1)} %get-tuple-element.26) | copy-start | bytes 25165828
  82.6 35.7 %copy-start.8 = (bf16[512,4,192]{0,2,1:T(8,128)(2,1)S(1)}, bf16[512,4,192]{0,2,1:T(8,128)(2,1)}, u32[]{:S(2)}) copy-start(bf16[512,4,192]{0,2,1:T(8,128)(2,1)} %slice.17) | copy-start | bytes 2359300
  118.3 1.5 copy-start.10
  119.9 6.1 %copy-start = (f32[4,512,1024]{2,1,0:T(8,128)}, f32[4,512,1024]{2,1,0:T(8,128)S(1)}, u32[]{:S(2)}) copy-start(f32[4,512,1024]{2,1,0:T(8,128)S(1)} %get-tuple-element.24) | copy-start | bytes 25165828
  121.4 4.6 %copy-start.1 = (f32[4,512,1024]{2,1,0:T(8,128)}, f32[4,512,1024]{2,1,0:T(8,128)S(1)}, u32[]{:S(2)}) copy-start(f32[4,512,1024]{2,1,0:T(8,128)S(1)} %get-tuple-element.28) | copy-start | bytes 25165828
  121.5 31.8 %copy-start.7 = (bf16[1024,4,128]{0,2,1:T(8,128)(2,1)S(1)}, bf16[1024,4,128]{0,2,1:T(8,128)(2,1)}, u32[]{:S(2)}) copy-start(bf16[1024,4,128]{0,2,1:T(8,128)(2,1)} %reshape.100) | copy-start | bytes 3145732
  170.2 7.6 %copy-start.11 = (bf16[192,1536]{1,0:T(8,128)(2,1)S(1)}, bf16[192,1536]{1,0:T(8,128)(2,1)}, u32[]{:S(2)}) copy-start(bf16[192,1536]{1,0:T(8,128)(2,1)} %param.8) | copy-start | bytes 1769476
  170.2 8.5 %copy-start.12 = (bf16[64,1024]{1,0:T(8,128)(2,1)S(1)}, bf16[64,1024]{1,0:T(8,128)(2,1)}, u32[]{:S(2)}) copy-start(bf16[64,1024]{1,0:T(8,128)(2,1)} %param.9) | copy-start | bytes 393220
where the time goes:
time: 181 us; the launch traced here: 180 us
  waiting for transfers between devices  55.5 us (31%)
  local copies, waits for them, and re-layouts  31.4 us (17%)
  matrix products  30.7 us (17%)
  blocking collectives  24.9 us (14%)
  starting transfers between devices  21.2 us (12%)
  other arithmetic  15.1 us (8%)
    ppermute x2, waiting for transfers between devices, shifted_2(): lax.ppermute(value, axis, [(source, source + steps) for source in range(f...  28.4 us
    dot_general x4, matrix products, partial_softmax(): jnp.einsum('htu,uhd->thd', rounded, value_cube, preferred_element_type=jn...  22 us
    all_to_all x1, waiting for transfers between devices, body(): lax.all_to_all(key_rows, 'head', split_axis=1, concat_axis=0, tiled=True)  16.1 us
    pmax x1, blocking collectives, body(): cycle_peak = lax.pmax(local_peak, 'ctx')  12.9 us
    unnamed x1, blocking collectives  12 us
    all_to_all x1, waiting for transfers between devices, body(): lax.all_to_all(value_rows, 'head', split_axis=1, concat_axis=0, tiled=True)  11 us
    dot_general x4, matrix products, head_scores(): jnp.einsum('thd,uhd->htu', query_cube, key_cube, preferred_element_type=j...  8.76 us
    unnamed x34, local copies, waits for them, and re-layouts  8.34 us
  transfers between devices with their start and end apart: 5, of which 3 were waited for; matrix products, arithmetic and copies ran while one was open for 25% of the time, Pallas kernels for 0%

commit v1 on v0

v1 whole, which is shorter than its diff:
```python
import functools
import math

import jax
import jax.numpy as jnp
from jax import lax
from jax.experimental import pallas as pl
from jax.experimental.pallas import tpu as pltpu
from jax.sharding import PartitionSpec as P


DNOPE = 128
DROPE = 64
DV = 128
DQK = 192
PAIR = 2 * DQK
WIDE = 256

clip_threshold = 100.0
SCALE = DQK ** (-0.5)
EXPO = SCALE * math.log2(math.e)


def after(value, *earlier):
    return lax.optimization_barrier((value,) + earlier)[0]


def to_next(value, ring=True):
    count = lax.axis_size("ctx")
    pairs = [(i, (i + 1) % count) for i in range(count if ring else count - 1)]
    return lax.ppermute(value, "ctx", pairs)


def swap(value, axis, step):
    count = lax.axis_size(axis)
    return lax.ppermute(value, axis, [(i, i ^ step) for i in range(count)])


def row_span(place_ref, step, rows):
    return pl.ds(pl.multiple_of((place_ref[0] ^ step) * rows, rows), rows)


def head_lanes(head):
    start = (head // 2) * PAIR + (head % 2) * (PAIR - WIDE)
    return slice(start, start + WIDE)


def keep_keys(piece, head):
    part = piece[:, head_lanes(head)]
    lane = lax.broadcasted_iota(jnp.int32, part.shape, 1)
    mask = (lane < DQK) if head % 2 == 0 else (lane >= WIDE - DQK)
    return jnp.where(mask, part, jnp.zeros_like(part))


def dot_keys(query, key):
    return lax.dot_general(
        query, key, (((1,), (1,)), ((), ())), preferred_element_type=jnp.float32
    )


def softmax_parts(scores, store):
    high = functools.reduce(jnp.maximum, scores).max(axis=1, keepdims=True)
    total = None
    for u, s in enumerate(scores):
        p = jnp.exp2((s - high) * EXPO)
        store(u, p.astype(jnp.bfloat16))
        total = p if total is None else total + p
    return high, total.sum(axis=1, keepdims=True)


def by_lane(columns):
    shape = (columns[0].shape[0], 128)
    lane = lax.broadcasted_iota(jnp.int32, shape, 1)
    packed = jnp.broadcast_to(columns[0], shape)
    for head in range(1, len(columns)):
        packed = jnp.where(lane == head, columns[head], packed)
    return packed


def from_lane(packed, head):
    return jnp.broadcast_to(packed[:, head : head + 1], (packed.shape[0], 128))


def cut_kernel(steps, place_ref, source_ref, *refs):
    pieces, sems = refs[:-1], refs[-1]
    width = pieces[0].shape[1]
    copies = []
    for at, (step, piece) in enumerate(zip(steps, pieces)):
        start = pl.multiple_of((place_ref[0] ^ step) * width, 128)
        copies.append(
            pltpu.make_async_copy(source_ref.at[:, pl.ds(start, width)], piece, sems.at[at])
        )
    for copy in copies:
        copy.start()
    for copy in copies:
        copy.wait()


def own_kernel(steps, fresh, place_ref, *refs):
    parts = len(steps)
    queries = refs[:parts]
    p_ref, high_ref, total_ref, key_ref, query_s = refs[-5:]
    heads, size, _ = p_ref.shape
    rows = queries[0].shape[0]
    count = size // rows
    if fresh:
        for step, piece in enumerate(refs[parts:-5]):
            for head in range(heads):
                key_ref[head, row_span(place_ref, step, rows), :] = keep_keys(piece, head)
    else:
        key_ref = refs[parts]
    for part in range(parts):
        query_s[part] = queries[part][...]
    below = lax.broadcasted_iota(jnp.int32, (rows, rows), 0) >= lax.broadcasted_iota(
        jnp.int32, (rows, rows), 1
    )

    def piece_step(part, carry):
        step = steps[0]
        for at in range(1, parts):
            step = jnp.where(part == at, steps[at], step)
        position = place_ref[0] ^ step
        for j in range(count):

            @pl.when(position == j)
            def _(j=j):
                span = slice(j * rows, (j + 1) * rows)
                highs, totals = [], []
                for head in range(heads):
                    query = query_s[part, :, head_lanes(head)]
                    scores = []
                    for u in range(j + 1):
                        s = dot_keys(query, key_ref[head, u * rows : (u + 1) * rows, :])
                        scores.append(jnp.where(below, s, -jnp.inf) if u == j else s)

                    def store(u, p, head=head):
                        p_ref[head, span, u * rows : (u + 1) * rows] = p

                    high, total = softmax_parts(scores, store)
                    highs.append(high)
                    totals.append(total)
                high_ref[span] = by_lane(highs)
                total_ref[span] = by_lane(totals)

        return carry

    lax.fori_loop(0, parts, piece_step, 0)


def far_kernel(steps, fresh, place_ref, *refs):
    parts = len(steps)
    queries = refs[:parts]
    p_ref, high_ref, total_ref, key_ref = refs[-4:]
    heads, _, width = p_ref.shape
    rows = queries[0].shape[0]
    if fresh:
        for at, piece in enumerate(refs[parts:-4]):
            for head in range(heads):
                key_ref[head, at * rows : (at + 1) * rows, :] = keep_keys(piece, head)
    else:
        key_ref = refs[parts]
    for step, piece in zip(steps, queries):
        span = row_span(place_ref, step, rows)
        highs, totals = [], []
        for head in range(heads):
            query = piece[:, head_lanes(head)]
            scores = [
                dot_keys(query, key_ref[head, u * rows : (u + 1) * rows, :])
                for u in range(width // rows)
            ]

            def store(u, p, head=head, span=span):
                p_ref[head, span, u * rows : (u + 1) * rows] = p

            high, total = softmax_parts(scores, store)
            highs.append(high)
            totals.append(total)
        high_ref[span] = by_lane(highs)
        total_ref[span] = by_lane(totals)


def merge_kernel(count, place_ref, *refs):
    queries, key = refs[:count], refs[count]
    own_high, own_total, far_high, far_total = refs[count + 1 : count + 5]
    p_ref, own_ref, far_ref, end_ref, peak_ref = refs[count + 5 :]
    heads, _, rows = p_ref.shape
    near = place_ref[1] > 0
    keys = [keep_keys(key, head) for head in range(heads)]
    peak = None
    for step, piece in enumerate(queries):
        span = row_span(place_ref, step, rows)
        highs, totals = [], []
        for head in range(heads):

            def store(u, p, head=head, span=span):
                p_ref[head, span] = p

            high, total = softmax_parts([dot_keys(piece[:, head_lanes(head)], keys[head])], store)
            highs.append(high)
            totals.append(total)
        end_high = jnp.where(near, by_lane(highs), -jnp.inf)
        far = jnp.where(near, far_high[span], -jnp.inf)
        own = own_high[span]
        top = jnp.maximum(own, jnp.maximum(far, end_high))
        own_scale = jnp.exp2((own - top) * EXPO)
        far_scale = jnp.exp2((far - top) * EXPO)
        end_scale = jnp.exp2((end_high - top) * EXPO)
        share = 1.0 / (
            own_scale * own_total[span] + far_scale * far_total[span] + end_scale * by_lane(totals)
        )
        own_ref[span] = own_scale * share
        far_ref[span] = far_scale * share
        end_ref[span] = end_scale * share
        best = jnp.max(top, axis=0, keepdims=True)
        peak = best if peak is None else jnp.maximum(peak, best)
    peak_ref[...] = jnp.broadcast_to(peak * SCALE, peak_ref.shape)


def mix_kernel(count, place_ref, *refs):
    own_values, far_values = refs[:count], refs[count : 2 * count - 1]
    p_own, p_far, own_ref, far_ref, out_ref, value_s = refs[2 * count - 1 :]
    rows = own_values[0].shape[0]
    for step, piece in enumerate(own_values):
        value_s[row_span(place_ref, step, rows), :] = piece[...]
    for head in range(p_own.shape[0]):
        lanes = slice(head * DV, (head + 1) * DV)
        for j in range(count):
            span = slice(j * rows, (j + 1) * rows)
            far = None
            for u, piece in enumerate(far_values):
                s = jnp.dot(
                    p_far[head, span, u * rows : (u + 1) * rows],
                    piece[:, lanes],
                    preferred_element_type=jnp.float32,
                )
                far = s if far is None else far + s
            keys = (j + 1) * rows
            own = jnp.dot(
                p_own[head, span, :keys], value_s[:keys, lanes], preferred_element_type=jnp.float32
            )
            out_ref[span, lanes] = own * from_lane(own_ref[span], head) + far * from_lane(
                far_ref[span], head
            )


def last_kernel(value_ref, p_ref, end_ref, sum_ref, out_ref):
    heads, size, rows = p_ref.shape
    for head in range(heads):
        lanes = slice(head * DV, (head + 1) * DV)
        for j in range(size // rows):
            span = slice(j * rows, (j + 1) * rows)
            far = jnp.dot(p_ref[head, span], value_ref[:, lanes], preferred_element_type=jnp.float32)
            out_ref[span, lanes] = (
                sum_ref[span, lanes] + far * from_lane(end_ref[span], head)
            ).astype(jnp.bfloat16)


def local_call(kernel, out_shape, place, operands, scratch=(), aliases=None, far=False):
    near = pl.BlockSpec(memory_space=pltpu.VMEM)
    specs = [pl.BlockSpec(memory_space=pltpu.HBM) if far else near] * len(operands)
    if place is not None:
        specs, operands = [pl.BlockSpec(memory_space=pltpu.SMEM)] + specs, [place] + operands
    return pl.pallas_call(
        kernel,
        out_shape=out_shape,
        in_specs=specs,
        out_specs=jax.tree.map(lambda _: near, out_shape),
        scratch_shapes=scratch,
        input_output_aliases=aliases or {},
        compiler_params=pltpu.CompilerParams(vmem_limit_bytes=8 << 20),
    )(*operands)


def cut(place, source, steps, count):
    shape = jax.ShapeDtypeStruct((source.shape[0], source.shape[1] // count), source.dtype)
    return local_call(
        functools.partial(cut_kernel, tuple(steps)),
        (shape,) * len(steps),
        place,
        [source],
        [pltpu.SemaphoreType.DMA((len(steps),))],
        far=True,
    )


def scores(kernel, place, steps, queries, keys, width, earlier, scratch):
    (rows, lanes), heads = queries[0].shape, queries[0].shape[1] // DQK
    total = lax.axis_size("head") * rows
    stat = jax.ShapeDtypeStruct((total, 128), jnp.float32)
    shapes = (jax.ShapeDtypeStruct((heads, total, width), jnp.bfloat16), stat, stat)
    prepared = jax.ShapeDtypeStruct((heads, width, WIDE), jnp.bfloat16)
    body = functools.partial(kernel, tuple(steps), earlier is None)
    if earlier is None:
        return local_call(body, shapes + (prepared,), place, [*queries, *keys], scratch)
    p, high, sums, ready = earlier
    first = len(queries) + 2
    aliases = {first: 0, first + 1: 1, first + 2: 2}
    operands = [*queries, ready, p, high, sums]

    def aliased(*refs):
        body(*refs[: first], *refs[first + 3 : first + 6], None, *refs[first + 6 :])

    return local_call(aliased, shapes, place, operands, scratch, aliases)


def own_scores(place, steps, queries, keys, earlier=None):
    rows, lanes = queries[0].shape
    width = rows * lax.axis_size("head")
    scratch = [pltpu.VMEM((len(steps), rows, lanes), jnp.bfloat16)]
    return scores(own_kernel, place, steps, queries, keys, width, earlier, scratch)


def far_scores(place, steps, queries, keys, earlier=None):
    width = queries[0].shape[0] * (lax.axis_size("head") - 1)
    return scores(far_kernel, place, steps, queries, keys, width, earlier, [])


def merge(place, queries, key, stats):
    count, (rows, lanes) = len(queries), key.shape
    stat = jax.ShapeDtypeStruct((count * rows, 128), jnp.float32)
    return local_call(
        functools.partial(merge_kernel, count),
        (
            jax.ShapeDtypeStruct((lanes // DQK, count * rows, rows), jnp.bfloat16),
            stat,
            stat,
            stat,
            jax.ShapeDtypeStruct((8, 128), jnp.float32),
        ),
        place,
        [*queries, key, *stats],
    )


def mix(place, own_values, far_values, parts):
    count, (rows, lanes) = len(own_values), own_values[0].shape
    return local_call(
        functools.partial(mix_kernel, count),
        jax.ShapeDtypeStruct((count * rows, lanes), jnp.float32),
        place,
        [*own_values, *far_values, *parts],
        [pltpu.VMEM((count * rows, lanes), jnp.bfloat16)],
    )


def last(value, p_end, end_share, partial):
    return local_call(
        last_kernel,
        jax.ShapeDtypeStruct(partial.shape, jnp.bfloat16),
        None,
        [value, p_end, end_share, partial],
    )


def top_kernel(*refs):
    refs[-1][...] = functools.reduce(jnp.maximum, [ref[...] for ref in refs[:-1]])


def top_of(parts):
    shape = jax.ShapeDtypeStruct(parts[0].shape, parts[0].dtype)
    return local_call(top_kernel, shape, None, list(parts))


def shared_peak(peak, axis):
    count = lax.axis_size(axis)
    if count <= 4:
        return top_of([peak] + [swap(peak, axis, step) for step in range(1, count)])
    step = 1
    while step < count:
        peak = top_of([peak, swap(peak, axis, step)])
        step *= 2
    return peak


def wanted_peaks(peak, wide):
    heads = lax.axis_size("head")
    cores = lax.axis_size("fsdp")
    found = []
    for turn in range(wide):
        pairs = []
        for head in range(heads):
            for core in range(cores):
                group = head * wide + (core + turn) % wide
                source = (group % heads) * cores + group // heads
                pairs.append((source, head * cores + core))
        found.append(lax.ppermute(peak, ("head", "fsdp"), pairs))
    return found


def clip_kernel(wide, place_ref, *refs):
    found, (query_ref, key_ref, query_out, key_out) = refs[:wide], refs[wide:]
    each = key_ref.shape[1] // DNOPE // wide
    lane = lax.broadcasted_iota(jnp.int32, (1, 128), 1)
    for slot in range(wide):
        peaks = found[0][:1, :]
        for turn in range(1, wide):
            peaks = jnp.where((place_ref[2] + turn) % wide == slot, found[turn][:1, :], peaks)
        factor = jnp.minimum(1.0, clip_threshold / peaks)
        root = jnp.sqrt(factor)
        for even in range(0, each, 2):
            full = [from_lane(factor, head) for head in (even, even + 1)]
            half = [from_lane(root, head) for head in (even, even + 1)]
            start = (slot * each + even) * DQK
            lanes_of = {
                start: half[0],
                start + 128: jnp.where(lane < DROPE, full[0], half[1]),
                start + 256: jnp.where(lane < DROPE, half[1], full[1]),
            }
            for at, row in lanes_of.items():
                part = query_ref[:, at : at + 128].astype(jnp.float32) * row
                query_out[:, at : at + 128] = part.astype(jnp.bfloat16)
            for odd in range(2):
                at = (slot * each + even + odd) * DNOPE
                part = key_ref[:, at : at + DNOPE].astype(jnp.float32) * half[odd]
                key_out[:, at : at + DNOPE] = part.astype(jnp.bfloat16)


def clip(place, found, query_weight, key_weight):
    return local_call(
        functools.partial(clip_kernel, len(found)),
        tuple(jax.ShapeDtypeStruct(w.shape, w.dtype) for w in (query_weight, key_weight)),
        place,
        [*found, query_weight, key_weight],
    )


def program(query_rows, key_rows, value_rows, query_weight, key_weight):
    count = lax.axis_size("head")
    steps = list(range(count))
    end = count - 1
    place = jnp.stack([lax.axis_index(name) for name in ("head", "ctx", "fsdp")]).astype(jnp.int32)

    def spread(pieces):
        return pieces[:1] + [swap(pieces[s], "head", s) for s in steps[1:]]

    def onward(pieces):
        return [to_next(pieces[s], s < end) for s in steps]

    key = spread(list(cut(place, key_rows, steps, count)))
    value = spread(list(cut(place, value_rows, steps, count)))
    query = spread(list(cut(place, query_rows, steps, count)))
    far_key, far_value = onward(key), onward(value)

    first, second = steps[: count // 2], steps[count // 2 :]
    *own, own_keys = own_scores(place, first, [query[s] for s in first], key)
    *far, far_keys = far_scores(place, first, [query[s] for s in first], far_key[:end])
    own = own_scores(place, second, [query[s] for s in second], None, (*own, own_keys))
    far = far_scores(place, second, [query[s] for s in second], None, (*far, far_keys))
    p_end, own_share, far_share, end_share, peaks = merge(
        place, query, far_key[end], [*own[1:], *far[1:]]
    )
    partial = mix(place, value, far_value[:end], [own[0], far[0], own_share, far_share])
    found = wanted_peaks(shared_peak(peaks, "ctx"), lax.axis_size("fsdp"))
    clipped_query, clipped_key = clip(place, found, query_weight, key_weight)
    partial = after(partial, clipped_query, clipped_key)
    attended = last(far_value[end], p_end, end_share, partial)
    return (attended, clipped_query, clipped_key)


def solution(mesh):
    return sharded(mesh)


def sharded(mesh):
    return jax.shard_map(
        program,
        mesh=mesh,
        in_specs=(
            P(("ctx", "head"), "fsdp"),
            P(("ctx", "head"), "fsdp"),
            P(("ctx", "head"), "fsdp"),
            P(("ctx", "fsdp"), "head"),
            P(("ctx", "fsdp"), "head"),
        ),
        out_specs=(
            P("ctx", ("fsdp", "head")),
            P(("ctx", "fsdp"), "head"),
            P(("ctx", "fsdp"), "head"),
        ),
        check_vma=False,
    )
```

time: 181 us -> 108 us (0.60)
  matrix products: 30.7 us -> 0 us
  local copies, waits for them, and re-layouts: 31.4 us -> 2.65 us
  blocking collectives: 24.9 us -> 0 us
  Pallas kernels: 0 us -> 22.4 us
  starting transfers between devices: 21.2 us -> 42.8 us
  waiting for transfers between devices: 55.5 us -> 38.3 us
  other arithmetic: 15.1 us -> 0.08 us
    ppermute x2 -> x22, starting transfers between devices: 8.16 us -> 42.8 us  [the longest x12 23.2 us: swap(): return lax.ppermute(value, axis, [(i, i ^ step) for i in range(count)])]
    dot_general x8 -> x0, matrix products: 30.7 us -> none  [the longest x4 22 us: partial_softmax(): jnp.einsum('htu,uhd->thd', rounded, value_cube, preferred_element_type=jn...]
    all_to_all x3 -> x0, waiting for transfers between devices: 27.2 us -> none  [the longest x1 16.1 us: body(): lax.all_to_all(key_rows, 'head', split_axis=1, concat_axis=0, tiled=True)]
    pallas_call x0 -> x12, Pallas kernels: none -> 22.4 us  [local_call(): pl.pallas_call(kernel, out_shape=out_shape, in_specs=specs, out_specs=jax...]
    all_to_all x3 -> x0, starting transfers between devices: 13.1 us -> none  [the longest x1 5.19 us: body(): lax.all_to_all(value_rows, 'head', split_axis=1, concat_axis=0, tiled=True)]
    pmax x1 -> x0, blocking collectives: 12.9 us -> none  [body(): cycle_peak = lax.pmax(local_peak, 'ctx')]
    unnamed x1 -> x0, blocking collectives: 12 us -> none
    reduce_max x2 -> x0, other arithmetic: 10.2 us -> none  [the longest x1 5.61 us: causal_block(): return (partial_softmax(scores, value_cube), jnp.max(scores, axis=(1, 2)))]
  transfers between devices with their start and end apart: 5 -> 22, of which waited for: 3 -> 10; matrix products, arithmetic and copies ran while one was open for 25% -> 0% of each run, Pallas kernels for 0% -> 19%
where the time goes in v1:
time: 108 us; the launch traced here: 107 us
  starting transfers between devices  42.8 us (40%)
  waiting for transfers between devices  38.3 us (35%)
  Pallas kernels  22.4 us (21%)
  local copies, waits for them, and re-layouts  2.65 us (2%)
    ppermute x12, waiting for transfers between devices, swap(): return lax.ppermute(value, axis, [(i, i ^ step) for i in range(count)])  37.2 us
    ppermute x12, starting transfers between devices, swap(): return lax.ppermute(value, axis, [(i, i ^ step) for i in range(count)])  23.2 us
    pallas_call x12, Pallas kernels, local_call(): pl.pallas_call(kernel, out_shape=out_shape, in_specs=specs, out_specs=jax...  22.4 us
    ppermute x8, starting transfers between devices, to_next(): return lax.ppermute(value, 'ctx', pairs)  16 us
    ppermute x2, starting transfers between devices, wanted_peaks(): found.append(lax.ppermute(peak, ('head', 'fsdp'), pairs))  3.59 us
    unnamed x10, local copies, waits for them, and re-layouts  2.65 us
  transfers between devices with their start and end apart: 22, of which 10 were waited for; matrix products, arithmetic and copies ran while one was open for 0% of the time, Pallas kernels for 19%

profile of v1, /device:TPU:0, one launch (start us, length us, event | category | flops | bytes accessed | tf_op | source)
XLA Modules:
  0.0 107.0 jit_solution(11973506509394995152)
XLA Ops:
  2.6 4.0 %collective-permute-start = (bf16[256,512]{1,0:T(8,128)(2,1)S(1)}, bf16[256,512]{1,0:T(8,128)(2,1)S(1)}, u32[]{:S(2)}, u32[]{:S(2)}) collective-permute-start(bf16[256,512]{1,0:T(8,128)(2,1)S(1)} %get-tuple-element.37), channel_id=1, source_target_pairs={{0,6},{2,4},{4,2},{6,0},{1,7},{3,5},{5,3},{7,1},{8,14},{10,12},{12... | collective-permute-start | bytes 786440 | tf_op jit(solution)/shard_map/ppermute | solution.py:36
  9.4 2.0 %collective-permute-start.2 = (bf16[256,768]{1,0:T(8,128)(2,1)S(1)}, bf16[256,768]{1,0:T(8,128)(2,1)S(1)}, u32[]{:S(2)}, u32[]{:S(2)}) collective-permute-start(bf16[256,768]{1,0:T(8,128)(2,1)S(1)} %get-tuple-element.39), channel_id=1, source_target_pairs={{0,2},{2,0},{4,6},{6,4},{1,3},{3,1},{5,7},{7,5},{8,10},{10,8},{12,... | collective-permute-start | bytes 1179656 | tf_op jit(solution)/shard_map/ppermute | solution.py:36
  13.8 2.0 %collective-permute-start.7 = (bf16[256,768]{1,0:T(8,128)(2,1)S(1)}, bf16[256,768]{1,0:T(8,128)(2,1)S(1)}, u32[]{:S(2)}, u32[]{:S(2)}) collective-permute-start(bf16[256,768]{1,0:T(8,128)(2,1)S(1)} %get-tuple-element.44), channel_id=1, source_target_pairs={{0,2},{2,0},{4,6},{6,4},{1,3},{3,1},{5,7},{7,5},{8,10},{10,8},{12,... | collective-permute-start | bytes 1179656 | tf_op jit(solution)/shard_map/ppermute | solution.py:36
  15.8 4.2 %collective-permute-done.12.refs_1_ = bf16[256,512]{1,0:T(8,128)(2,1)S(1)} collective-permute-done((bf16[256,512]{1,0:T(8,128)(2,1)S(1)}, bf16[256,512]{1,0:T(8,128)(2,1)S(1)}, u32[]{:S(2)}, u32[]{:S(2)}) %collective-permute-start.12) | collective-permute-done | bytes 262176 | tf_op jit(solution)/shard_map/ppermute | solution.py:36
  20.0 2.9 %collective-permute-start.5 = (bf16[256,768]{1,0:T(8,128)(2,1)S(1)}, bf16[256,768]{1,0:T(8,128)(2,1)S(1)}, u32[]{:S(2)}, u32[]{:S(2)}) collective-permute-start(bf16[256,768]{1,0:T(8,128)(2,1)S(1)} %get-tuple-element.42), channel_id=1, source_target_pairs={{0,6},{2,4},{4,2},{6,0},{1,7},{3,5},{5,3},{7,1},{8,14},{10,12},{12... | collective-permute-start | bytes 1179656 | tf_op jit(solution)/shard_map/ppermute | solution.py:36
  22.9 5.5 %collective-permute-done.2.refs_1_ = bf16[256,768]{1,0:T(8,128)(2,1)S(1)} collective-permute-done((bf16[256,768]{1,0:T(8,128)(2,1)S(1)}, bf16[256,768]{1,0:T(8,128)(2,1)S(1)}, u32[]{:S(2)}, u32[]{:S(2)}) %collective-permute-start.2) | collective-permute-done | bytes 393248 | tf_op jit(solution)/shard_map/ppermute | solution.py:36
  29.8 1.6 %collective-permute-start.9 = (bf16[256,768]{1,0:T(8,128)(2,1)S(1)}, bf16[256,768]{1,0:T(8,128)(2,1)S(1)}, u32[]{:S(2)}, u32[]{:S(2)}) collective-permute-start(bf16[256,768]{1,0:T(8,128)(2,1)S(1)} %get-tuple-element.43.refs_2_), channel_id=1, source_target_pairs={{0,8},{8,16},{16,24},{24,0},{1,9},{9,17},{17,25},{25,1},{2,10},{10... | collective-permute-start | bytes 1179656 | tf_op jit(solution)/shard_map/ppermute | solution.py:31
  31.4 5.4 %collective-permute-done.7.refs_3_ = bf16[256,768]{1,0:T(8,128)(2,1)S(1)} collective-permute-done((bf16[256,768]{1,0:T(8,128)(2,1)S(1)}, bf16[256,768]{1,0:T(8,128)(2,1)S(1)}, u32[]{:S(2)}, u32[]{:S(2)}) %collective-permute-start.7) | collective-permute-done | bytes 393248 | tf_op jit(solution)/shard_map/ppermute | solution.py:36
  36.8 1.6 %collective-permute-start.10 = (bf16[256,768]{1,0:T(8,128)(2,1)S(1)}, bf16[256,768]{1,0:T(8,128)(2,1)S(1)}, u32[]{:S(2)}, u32[]{:S(2)}) collective-permute-start(bf16[256,768]{1,0:T(8,128)(2,1)S(1)} %collective-permute-done.7.refs_3_), channel_id=1, source_target_pairs={{0,8},{8,16},{16,24},{24,0},{1,9},{9,17},{17,25},{25,1},{2,10},{10... | collective-permute-start | bytes 1179656 | tf_op jit(solution)/shard_map/ppermute | solution.py:31
  38.4 1.6 %collective-permute-start.11 = (bf16[256,768]{1,0:T(8,128)(2,1)S(1)}, bf16[256,768]{1,0:T(8,128)(2,1)S(1)}, u32[]{:S(2)}, u32[]{:S(2)}) collective-permute-start(bf16[256,768]{1,0:T(8,128)(2,1)S(1)} %collective-permute-done.8.refs_4_), channel_id=1, source_target_pairs={{0,8},{8,16},{16,24},{24,0},{1,9},{9,17},{17,25},{25,1},{2,10},{10... | collective-permute-start | bytes 1179656 | tf_op jit(solution)/shard_map/ppermute | solution.py:31
  40.0 4.7 %collective-permute-done.5.refs_5_ = bf16[256,768]{1,0:T(8,128)(2,1)S(1)} collective-permute-done((bf16[256,768]{1,0:T(8,128)(2,1)S(1)}, bf16[256,768]{1,0:T(8,128)(2,1)S(1)}, u32[]{:S(2)}, u32[]{:S(2)}) %collective-permute-start.5) | collective-permute-done | bytes 393248 | tf_op jit(solution)/shard_map/ppermute | solution.py:36
  44.7 4.0 %collective-permute-start.6 = (bf16[256,768]{1,0:T(8,128)(2,1)S(1)}, bf16[256,768]{1,0:T(8,128)(2,1)S(1)}, u32[]{:S(2)}, u32[]{:S(2)}) collective-permute-start(bf16[256,768]{1,0:T(8,128)(2,1)S(1)} %collective-permute-done.5.refs_5_), channel_id=1, source_target_pairs={{0,8},{8,16},{16,24},{1,9},{9,17},{17,25},{2,10},{10,18},{18,26},{... | collective-permute-start | bytes 1179656 | tf_op jit(solution)/shard_map/ppermute | solution.py:31
  48.7 3.6 %collective-permute-done.4.refs_2_.refs_3_ = bf16[256,768]{1,0:T(8,128)(2,1)S(1)} collective-permute-done((bf16[256,768]{1,0:T(8,128)(2,1)S(1)}, bf16[256,768]{1,0:T(8,128)(2,1)S(1)}, u32[]{:S(2)}, u32[]{:S(2)}) %collective-permute-start.4) | collective-permute-done | bytes 393248 | tf_op jit(solution)/shard_map/ppermute | solution.py:36
  52.3 1.8 %collective-permute-start.14 = (bf16[256,512]{1,0:T(8,128)(2,1)S(1)}, bf16[256,512]{1,0:T(8,128)(2,1)S(1)}, u32[]{:S(2)}, u32[]{:S(2)}) collective-permute-start(bf16[256,512]{1,0:T(8,128)(2,1)S(1)} %get-tuple-element.60.refs_0_), channel_id=1, source_target_pairs={{0,8},{8,16},{16,24},{24,0},{1,9},{9,17},{17,25},{25,1},{2,10},{10... | collective-permute-start | bytes 786440 | tf_op jit(solution)/shard_map/ppermute | solution.py:31
  54.0 1.6 %collective-permute-start.15 = (bf16[256,512]{1,0:T(8,128)(2,1)S(1)}, bf16[256,512]{1,0:T(8,128)(2,1)S(1)}, u32[]{:S(2)}, u32[]{:S(2)}) collective-permute-start(bf16[256,512]{1,0:T(8,128)(2,1)S(1)} %collective-permute-done.12.refs_1_), channel_id=1, source_target_pairs={{0,8},{8,16},{16,24},{24,0},{1,9},{9,17},{17,25},{25,1},{2,10},{10... | collective-permute-start | bytes 786440 | tf_op jit(solution)/shard_map/ppermute | solution.py:31
  55.6 1.6 %collective-permute-start.16 = (bf16[256,512]{1,0:T(8,128)(2,1)S(1)}, bf16[256,512]{1,0:T(8,128)(2,1)S(1)}, u32[]{:S(2)}, u32[]{:S(2)}) collective-permute-start(bf16[256,512]{1,0:T(8,128)(2,1)S(1)} %collective-permute-done.13.refs_2_), channel_id=1, source_target_pairs={{0,8},{8,16},{16,24},{24,0},{1,9},{9,17},{17,25},{25,1},{2,10},{10... | collective-permute-start | bytes 786440 | tf_op jit(solution)/shard_map/ppermute | solution.py:31
  58.3 2.4 %collective-permute-start.1 = (bf16[256,512]{1,0:T(8,128)(2,1)S(1)}, bf16[256,512]{1,0:T(8,128)(2,1)S(1)}, u32[]{:S(2)}, u32[]{:S(2)}) collective-permute-start(bf16[256,512]{1,0:T(8,128)(2,1)S(1)} %collective-permute-done.refs_3_), channel_id=1, source_target_pairs={{0,8},{8,16},{16,24},{1,9},{9,17},{17,25},{2,10},{10,18},{18,26},{... | collective-permute-start | bytes 786440 | tf_op jit(solution)/shard_map/ppermute | solution.py:31
  60.7 2.1 %shard_map.79 = (bf16[4,1024,1024]{2,1,0:T(8,128)(2,1)S(1)}, f32[1024,128]{1,0:T(8,128)S(1)}, f32[1024,128]{1,0:T(8,128)S(1)}, bf16[4,1024,256]{2,1,0:T(8,128)(2,1)S(1)}) custom-call(s32[3]{0:T(128)S(1)} %pad_add_fusion.place_ref.refs_0_, bf16[256,768]{1,0:T(8,128)(2,1)S(1)} %get-tuple-element.38.refs_0_, ...), custom_call_target="tpu_custom_call" | custom-call | tf_op jit(solution)/shard_map/pallas_call | solution.py:263
  62.8 3.2 %shard_map.80 = (bf16[4,1024,1024]{2,1,0:T(8,128)(2,1)S(1)}, f32[1024,128]{1,0:T(8,128)S(1)}, f32[1024,128]{1,0:T(8,128)S(1)}) custom-call(s32[3]{0:T(128)S(1)} %pad_add_fusion.place_ref.refs_0_, bf16[256,768]{1,0:T(8,128)(2,1)S(1)} %collective-permute-done.3.refs_1_.refs_2_, ...), custom_call_target="tpu_custom_call", output_to_operand_aliasing={{0}: (4, {}), {1}: (5, {}), {2}: (6, {})} | custom-call | tf_op jit(solution)/shard_map/pallas_call | solution.py:263
  66.0 2.5 %shard_map.81 = (bf16[4,1024,768]{2,1,0:T(8,128)(2,1)S(1)}, f32[1024,128]{1,0:T(8,128)S(1)}, f32[1024,128]{1,0:T(8,128)S(1)}, bf16[4,768,256]{2,1,0:T(8,128)(2,1)S(1)}) custom-call(s32[3]{0:T(128)S(1)} %pad_add_fusion.place_ref.refs_0_, bf16[256,768]{1,0:T(8,128)(2,1)S(1)} %get-tuple-element.38.refs_0_, bf16[256,768]{1,0:T(8,128)(2,1)S(1)} %collective-permute-done.2.refs_1_, ...), custom_call_target="tpu_custom_call" | custom-call | tf_op jit(solution)/shard_map/pallas_call | solution.py:263
  68.4 2.5 %shard_map.82 = (bf16[4,1024,768]{2,1,0:T(8,128)(2,1)S(1)}, f32[1024,128]{1,0:T(8,128)S(1)}, f32[1024,128]{1,0:T(8,128)S(1)}) custom-call(s32[3]{0:T(128)S(1)} %pad_add_fusion.place_ref.refs_0_, bf16[256,768]{1,0:T(8,128)(2,1)S(1)} %collective-permute-done.3.refs_1_.refs_2_, ...), custom_call_target="tpu_custom_call", output_to_operand_aliasing={{0}: (4, {}), {1}: (5, {}), {2}: (6, {})} | custom-call | tf_op jit(solution)/shard_map/pallas_call | solution.py:263
  70.9 2.7 %shard_map.83 = (bf16[4,1024,256]{2,1,0:T(8,128)(2,1)S(1)}, f32[1024,128]{1,0:T(8,128)S(1)}, f32[1024,128]{1,0:T(8,128)S(1)}, f32[1024,128]{1,0:T(8,128)S(1)}, f32[8,128]{1,0:T(8,128)S(1)}) custom-call(s32[3]{0:T(128)S(1)} %pad_add_fusion.place_ref.refs_0_, bf16[256,768]{1,0:T(8,128)(2,1)S(1)} %get-tuple-element.38.refs_0_, ...), custom_call_target="tpu_custom_call" | custom-call | tf_op jit(solution)/shard_map/pallas_call | solution.py:263
  73.6 1.6 %collective-permute-start.17 = (f32[8,128]{1,0:T(8,128)S(1)}, f32[8,128]{1,0:T(8,128)S(1)}, u32[]{:S(2)}, u32[]{:S(2)}) collective-permute-start(f32[8,128]{1,0:T(8,128)S(1)} %get-tuple-element.67.refs_0_), channel_id=1, source_target_pairs={{0,8},{8,0},{16,24},{24,16},{1,9},{9,1},{17,25},{25,17},{2,10},{10... | collective-permute-start | bytes 12296 | tf_op jit(solution)/shard_map/ppermute | solution.py:36
  75.3 10.1 %collective-permute-done.17.refs_1_ = f32[8,128]{1,0:T(8,128)S(1)} collective-permute-done((f32[8,128]{1,0:T(8,128)S(1)}, f32[8,128]{1,0:T(8,128)S(1)}, u32[]{:S(2)}, u32[]{:S(2)}) %collective-permute-start.17) | collective-permute-done | bytes 4128 | tf_op jit(solution)/shard_map/ppermute | solution.py:36
  85.3 2.6 %collective-permute-start.18 = (f32[8,128]{1,0:T(8,128)S(1)}, f32[8,128]{1,0:T(8,128)S(1)}, u32[]{:S(2)}, u32[]{:S(2)}) collective-permute-start(f32[8,128]{1,0:T(8,128)S(1)} %get-tuple-element.67.refs_0_), channel_id=1, source_target_pairs={{0,16},{8,24},{16,0},{24,8},{1,17},{9,25},{17,1},{25,9},{2,18},{10... | collective-permute-start | bytes 12296 | tf_op jit(solution)/shard_map/ppermute | solution.py:36
  87.9 1.9 %collective-permute-done.18.refs_2_ = f32[8,128]{1,0:T(8,128)S(1)} collective-permute-done((f32[8,128]{1,0:T(8,128)S(1)}, f32[8,128]{1,0:T(8,128)S(1)}, u32[]{:S(2)}, u32[]{:S(2)}) %collective-permute-start.18) | collective-permute-done | bytes 4128 | tf_op jit(solution)/shard_map/ppermute | solution.py:36
  89.8 4.5 %collective-permute-start.19 = (f32[8,128]{1,0:T(8,128)S(1)}, f32[8,128]{1,0:T(8,128)S(1)}, u32[]{:S(2)}, u32[]{:S(2)}) collective-permute-start(f32[8,128]{1,0:T(8,128)S(1)} %get-tuple-element.67.refs_0_), channel_id=1, source_target_pairs={{0,24},{8,16},{16,8},{24,0},{1,25},{9,17},{17,9},{25,1},{2,26},{10... | collective-permute-start | bytes 12296 | tf_op jit(solution)/shard_map/ppermute | solution.py:36
  94.4 1.6 %collective-permute-done.19.refs_3_ = f32[8,128]{1,0:T(8,128)S(1)} collective-permute-done((f32[8,128]{1,0:T(8,128)S(1)}, f32[8,128]{1,0:T(8,128)S(1)}, u32[]{:S(2)}, u32[]{:S(2)}) %collective-permute-start.19) | collective-permute-done | bytes 4128 | tf_op jit(solution)/shard_map/ppermute | solution.py:36
  96.6 2.9 %collective-permute-start.21 = (f32[8,128]{1,0:T(8,128)S(1)}, f32[8,128]{1,0:T(8,128)S(1)}, u32[]{:S(2)}, u32[]{:S(2)}) collective-permute-start(f32[8,128]{1,0:T(8,128)S(1)} %shard_map.85), channel_id=1, source_target_pairs={{2,0},{0,1},{6,2},{4,3},{3,4},{1,5},{7,6},{5,7},{10,8},{8,9},{14,1... | collective-permute-start | bytes 12296 | tf_op jit(solution)/shard_map/ppermute | solution.py:386
  99.6 3.9 %shard_map.84.sum_ref = f32[1024,512]{1,0:T(8,128)S(1)} custom-call(s32[3]{0:T(128)S(1)} %pad_add_fusion.place_ref.refs_0_, bf16[256,512]{1,0:T(8,128)(2,1)S(1)} %get-tuple-element.60.refs_0_, bf16[256,512]{1,0:T(8,128)(2,1)S(1)} %collective-permute-done.12.refs_1_, bf16[256,512]{1,0:T(8,128)(2,1)S(1)} %collective-permute-done.13.refs_2_, ...), custom_call_target="tpu_custom_call" | custom-call | tf_op jit(solution)/shard_map/pallas_call | solution.py:263
  103.6 1.6 %shard_map.86 = (bf16[192,1536]{1,0:T(8,128)(2,1)}, bf16[64,1024]{1,0:T(8,128)(2,1)}) custom-call(s32[3]{0:T(128)S(1)} %pad_add_fusion.place_ref.refs_0_, f32[8,128]{1,0:T(8,128)S(1)} %collective-permute-done.20.refs_0_, f32[8,128]{1,0:T(8,128)S(1)} %collective-permute-done.21.refs_1_, bf16[192,1536]{1,0:T(8,128)(2,1)S(1)} %copy-done.3, ...), custom_call_target="tpu_custom_call" | custom-call | tf_op jit(solution)/shard_map/pallas_call | solution.py:263
  105.2 1.8 %shard_map.87 = bf16[1024,512]{1,0:T(8,128)(2,1)} custom-call(bf16[256,512]{1,0:T(8,128)(2,1)S(1)} %collective-permute-done.1.value_ref, bf16[4,1024,256]{2,1,0:T(8,128)(2,1)S(1)} %get-tuple-element.58.p_ref, f32[1024,128]{1,0:T(8,128)S(1)} %get-tuple-element.59.end_ref, f32[1024,512]{1,0:T(8,128)S(1)} %shard_map.84.sum_ref), custom_call_target="tpu_custom_call" | custom-call | tf_op jit(solution)/shard_map/pallas_call | solution.py:263
  (35 shorter events, 10.5 us)
Async XLA Ops:
  0.7 1.2 %copy-start.2 = (bf16[256,2048]{1,0:T(8,128)(2,1)S(1)}, bf16[256,2048]{1,0:T(8,128)(2,1)}, u32[]{:S(2)}) copy-start(bf16[256,2048]{1,0:T(8,128)(2,1)} %source_ref.3) | copy-start | bytes 3145732
  2.6 11.2 %collective-permute-start = (bf16[256,512]{1,0:T(8,128)(2,1)S(1)}, bf16[256,512]{1,0:T(8,128)(2,1)S(1)}, u32[]{:S(2)}, u32[]{:S(2)}) collective-permute-start(bf16[256,512]{1,0:T(8,128)(2,1)S(1)} %get-tuple-element.37), channel_id=1, source_target_pairs={{0,6},{2,4},{4,2},{6,0},{1,7},{3,5},{5,3},{7,1},{8,14},{10,12},{12... | collective-permute-start | bytes 786440 | tf_op jit(solution)/shard_map/ppermute | solution.py:36
  6.6 13.3 %collective-permute-start.12 = (bf16[256,512]{1,0:T(8,128)(2,1)S(1)}, bf16[256,512]{1,0:T(8,128)(2,1)S(1)}, u32[]{:S(2)}, u32[]{:S(2)}) collective-permute-start(bf16[256,512]{1,0:T(8,128)(2,1)S(1)} %get-tuple-element.61), channel_id=1, source_target_pairs={{0,2},{2,0},{4,6},{6,4},{1,3},{3,1},{5,7},{7,5},{8,10},{10,8},{12,... | collective-permute-start | bytes 786440 | tf_op jit(solution)/shard_map/ppermute | solution.py:36
  7.1 12.8 %collective-permute-start.13 = (bf16[256,512]{1,0:T(8,128)(2,1)S(1)}, bf16[256,512]{1,0:T(8,128)(2,1)S(1)}, u32[]{:S(2)}, u32[]{:S(2)}) collective-permute-start(bf16[256,512]{1,0:T(8,128)(2,1)S(1)} %get-tuple-element.62), channel_id=1, source_target_pairs={{0,4},{2,6},{4,0},{6,2},{1,5},{3,7},{5,1},{7,3},{8,12},{10,14},{12... | collective-permute-start | bytes 786440 | tf_op jit(solution)/shard_map/ppermute | solution.py:36
  7.2 1.4 %copy-start = (bf16[256,3072]{1,0:T(8,128)(2,1)S(1)}, bf16[256,3072]{1,0:T(8,128)(2,1)}, u32[]{:S(2)}) copy-start(bf16[256,3072]{1,0:T(8,128)(2,1)} %source_ref.4) | copy-start | bytes 4718596
  8.7 4.2 %copy-start.1 = (bf16[256,3072]{1,0:T(8,128)(2,1)S(1)}, bf16[256,3072]{1,0:T(8,128)(2,1)}, u32[]{:S(2)}) copy-start(bf16[256,3072]{1,0:T(8,128)(2,1)} %source_ref.5) | copy-start | bytes 4718596
  9.4 19.0 %collective-permute-start.2 = (bf16[256,768]{1,0:T(8,128)(2,1)S(1)}, bf16[256,768]{1,0:T(8,128)(2,1)S(1)}, u32[]{:S(2)}, u32[]{:S(2)}) collective-permute-start(bf16[256,768]{1,0:T(8,128)(2,1)S(1)} %get-tuple-element.39), channel_id=1, source_target_pairs={{0,2},{2,0},{4,6},{6,4},{1,3},{3,1},{5,7},{7,5},{8,10},{10,8},{12,... | collective-permute-start | bytes 1179656 | tf_op jit(solution)/shard_map/ppermute | solution.py:36
  11.4 18.5 %collective-permute-start.3 = (bf16[256,768]{1,0:T(8,128)(2,1)S(1)}, bf16[256,768]{1,0:T(8,128)(2,1)S(1)}, u32[]{:S(2)}, u32[]{:S(2)}) collective-permute-start(bf16[256,768]{1,0:T(8,128)(2,1)S(1)} %get-tuple-element.40), channel_id=1, source_target_pairs={{0,4},{2,6},{4,0},{6,2},{1,5},{3,7},{5,1},{7,3},{8,12},{10,14},{12... | collective-permute-start | bytes 1179656 | tf_op jit(solution)/shard_map/ppermute | solution.py:36
  13.8 23.0 %collective-permute-start.7 = (bf16[256,768]{1,0:T(8,128)(2,1)S(1)}, bf16[256,768]{1,0:T(8,128)(2,1)S(1)}, u32[]{:S(2)}, u32[]{:S(2)}) collective-permute-start(bf16[256,768]{1,0:T(8,128)(2,1)S(1)} %get-tuple-element.44), channel_id=1, source_target_pairs={{0,2},{2,0},{4,6},{6,4},{1,3},{3,1},{5,7},{7,5},{8,10},{10,8},{12,... | collective-permute-start | bytes 1179656 | tf_op jit(solution)/shard_map/ppermute | solution.py:36
  19.9 18.4 %collective-permute-start.8 = (bf16[256,768]{1,0:T(8,128)(2,1)S(1)}, bf16[256,768]{1,0:T(8,128)(2,1)S(1)}, u32[]{:S(2)}, u32[]{:S(2)}) collective-permute-start(bf16[256,768]{1,0:T(8,128)(2,1)S(1)} %get-tuple-element.45), channel_id=1, source_target_pairs={{0,4},{2,6},{4,0},{6,2},{1,5},{3,7},{5,1},{7,3},{8,12},{10,14},{12... | collective-permute-start | bytes 1179656 | tf_op jit(solution)/shard_map/ppermute | solution.py:36
  20.0 24.7 %collective-permute-start.5 = (bf16[256,768]{1,0:T(8,128)(2,1)S(1)}, bf16[256,768]{1,0:T(8,128)(2,1)S(1)}, u32[]{:S(2)}, u32[]{:S(2)}) collective-permute-start(bf16[256,768]{1,0:T(8,128)(2,1)S(1)} %get-tuple-element.42), channel_id=1, source_target_pairs={{0,6},{2,4},{4,2},{6,0},{1,7},{3,5},{5,3},{7,1},{8,14},{10,12},{12... | collective-permute-start | bytes 1179656 | tf_op jit(solution)/shard_map/ppermute | solution.py:36
  28.4 23.9 %collective-permute-start.4 = (bf16[256,768]{1,0:T(8,128)(2,1)S(1)}, bf16[256,768]{1,0:T(8,128)(2,1)S(1)}, u32[]{:S(2)}, u32[]{:S(2)}) collective-permute-start(bf16[256,768]{1,0:T(8,128)(2,1)S(1)} %get-tuple-element.41), channel_id=1, source_target_pairs={{0,6},{2,4},{4,2},{6,0},{1,7},{3,5},{5,3},{7,1},{8,14},{10,12},{12... | collective-permute-start | bytes 1179656 | tf_op jit(solution)/shard_map/ppermute | solution.py:36
  29.8 24.2 %collective-permute-start.9 = (bf16[256,768]{1,0:T(8,128)(2,1)S(1)}, bf16[256,768]{1,0:T(8,128)(2,1)S(1)}, u32[]{:S(2)}, u32[]{:S(2)}) collective-permute-start(bf16[256,768]{1,0:T(8,128)(2,1)S(1)} %get-tuple-element.43.refs_2_), channel_id=1, source_target_pairs={{0,8},{8,16},{16,24},{24,0},{1,9},{9,17},{17,25},{25,1},{2,10},{10... | collective-permute-start | bytes 1179656 | tf_op jit(solution)/shard_map/ppermute | solution.py:31
  36.8 18.8 %collective-permute-start.10 = (bf16[256,768]{1,0:T(8,128)(2,1)S(1)}, bf16[256,768]{1,0:T(8,128)(2,1)S(1)}, u32[]{:S(2)}, u32[]{:S(2)}) collective-permute-start(bf16[256,768]{1,0:T(8,128)(2,1)S(1)} %collective-permute-done.7.refs_3_), channel_id=1, source_target_pairs={{0,8},{8,16},{16,24},{24,0},{1,9},{9,17},{17,25},{25,1},{2,10},{10... | collective-permute-start | bytes 1179656 | tf_op jit(solution)/shard_map/ppermute | solution.py:31
  38.4 19.9 %collective-permute-start.11 = (bf16[256,768]{1,0:T(8,128)(2,1)S(1)}, bf16[256,768]{1,0:T(8,128)(2,1)S(1)}, u32[]{:S(2)}, u32[]{:S(2)}) collective-permute-start(bf16[256,768]{1,0:T(8,128)(2,1)S(1)} %collective-permute-done.8.refs_4_), channel_id=1, source_target_pairs={{0,8},{8,16},{16,24},{24,0},{1,9},{9,17},{17,25},{25,1},{2,10},{10... | collective-permute-start | bytes 1179656 | tf_op jit(solution)/shard_map/ppermute | solution.py:31
  44.7 26.2 %collective-permute-start.6 = (bf16[256,768]{1,0:T(8,128)(2,1)S(1)}, bf16[256,768]{1,0:T(8,128)(2,1)S(1)}, u32[]{:S(2)}, u32[]{:S(2)}) collective-permute-start(bf16[256,768]{1,0:T(8,128)(2,1)S(1)} %collective-permute-done.5.refs_5_), channel_id=1, source_target_pairs={{0,8},{8,16},{16,24},{1,9},{9,17},{17,25},{2,10},{10,18},{18,26},{... | collective-permute-start | bytes 1179656 | tf_op jit(solution)/shard_map/ppermute | solution.py:31
  52.3 44.3 %collective-permute-start.14 = (bf16[256,512]{1,0:T(8,128)(2,1)S(1)}, bf16[256,512]{1,0:T(8,128)(2,1)S(1)}, u32[]{:S(2)}, u32[]{:S(2)}) collective-permute-start(bf16[256,512]{1,0:T(8,128)(2,1)S(1)} %get-tuple-element.60.refs_0_), channel_id=1, source_target_pairs={{0,8},{8,16},{16,24},{24,0},{1,9},{9,17},{17,25},{25,1},{2,10},{10... | collective-permute-start | bytes 786440 | tf_op jit(solution)/shard_map/ppermute | solution.py:31
  54.0 45.5 %collective-permute-start.15 = (bf16[256,512]{1,0:T(8,128)(2,1)S(1)}, bf16[256,512]{1,0:T(8,128)(2,1)S(1)}, u32[]{:S(2)}, u32[]{:S(2)}) collective-permute-start(bf16[256,512]{1,0:T(8,128)(2,1)S(1)} %collective-permute-done.12.refs_1_), channel_id=1, source_target_pairs={{0,8},{8,16},{16,24},{24,0},{1,9},{9,17},{17,25},{25,1},{2,10},{10... | collective-permute-start | bytes 786440 | tf_op jit(solution)/shard_map/ppermute | solution.py:31
  55.6 43.9 %collective-permute-start.16 = (bf16[256,512]{1,0:T(8,128)(2,1)S(1)}, bf16[256,512]{1,0:T(8,128)(2,1)S(1)}, u32[]{:S(2)}, u32[]{:S(2)}) collective-permute-start(bf16[256,512]{1,0:T(8,128)(2,1)S(1)} %collective-permute-done.13.refs_2_), channel_id=1, source_target_pairs={{0,8},{8,16},{16,24},{24,0},{1,9},{9,17},{17,25},{25,1},{2,10},{10... | collective-permute-start | bytes 786440 | tf_op jit(solution)/shard_map/ppermute | solution.py:31
  58.3 46.9 %collective-permute-start.1 = (bf16[256,512]{1,0:T(8,128)(2,1)S(1)}, bf16[256,512]{1,0:T(8,128)(2,1)S(1)}, u32[]{:S(2)}, u32[]{:S(2)}) collective-permute-start(bf16[256,512]{1,0:T(8,128)(2,1)S(1)} %collective-permute-done.refs_3_), channel_id=1, source_target_pairs={{0,8},{8,16},{16,24},{1,9},{9,17},{17,25},{2,10},{10,18},{18,26},{... | collective-permute-start | bytes 786440 | tf_op jit(solution)/shard_map/ppermute | solution.py:31
  73.6 11.7 %collective-permute-start.17 = (f32[8,128]{1,0:T(8,128)S(1)}, f32[8,128]{1,0:T(8,128)S(1)}, u32[]{:S(2)}, u32[]{:S(2)}) collective-permute-start(f32[8,128]{1,0:T(8,128)S(1)} %get-tuple-element.67.refs_0_), channel_id=1, source_target_pairs={{0,8},{8,0},{16,24},{24,16},{1,9},{9,1},{17,25},{25,17},{2,10},{10... | collective-permute-start | bytes 12296 | tf_op jit(solution)/shard_map/ppermute | solution.py:36
  85.3 4.5 %collective-permute-start.18 = (f32[8,128]{1,0:T(8,128)S(1)}, f32[8,128]{1,0:T(8,128)S(1)}, u32[]{:S(2)}, u32[]{:S(2)}) collective-permute-start(f32[8,128]{1,0:T(8,128)S(1)} %get-tuple-element.67.refs_0_), channel_id=1, source_target_pairs={{0,16},{8,24},{16,0},{24,8},{1,17},{9,25},{17,1},{25,9},{2,18},{10... | collective-permute-start | bytes 12296 | tf_op jit(solution)/shard_map/ppermute | solution.py:36
  89.8 6.1 %collective-permute-start.19 = (f32[8,128]{1,0:T(8,128)S(1)}, f32[8,128]{1,0:T(8,128)S(1)}, u32[]{:S(2)}, u32[]{:S(2)}) collective-permute-start(f32[8,128]{1,0:T(8,128)S(1)} %get-tuple-element.67.refs_0_), channel_id=1, source_target_pairs={{0,24},{8,16},{16,8},{24,0},{1,25},{9,17},{17,9},{25,1},{2,26},{10... | collective-permute-start | bytes 12296 | tf_op jit(solution)/shard_map/ppermute | solution.py:36
  95.9 7.6 %collective-permute-start.20 = (f32[8,128]{1,0:T(8,128)S(1)}, f32[8,128]{1,0:T(8,128)S(1)}, u32[]{:S(2)}, u32[]{:S(2)}) collective-permute-start(f32[8,128]{1,0:T(8,128)S(1)} %shard_map.85), channel_id=1, source_target_pairs={{0,0},{2,1},{4,2},{6,3},{1,4},{3,5},{5,6},{7,7},{8,8},{10,9},{12,1... | collective-permute-start | bytes 12296 | tf_op jit(solution)/shard_map/ppermute | solution.py:386
  96.6 6.9 %collective-permute-start.21 = (f32[8,128]{1,0:T(8,128)S(1)}, f32[8,128]{1,0:T(8,128)S(1)}, u32[]{:S(2)}, u32[]{:S(2)}) collective-permute-start(f32[8,128]{1,0:T(8,128)S(1)} %shard_map.85), channel_id=1, source_target_pairs={{2,0},{0,1},{6,2},{4,3},{3,4},{1,5},{7,6},{5,7},{10,8},{8,9},{14,1... | collective-permute-start | bytes 12296 | tf_op jit(solution)/shard_map/ppermute | solution.py:386
  99.6 4.0 %copy-start.3 = (bf16[192,1536]{1,0:T(8,128)(2,1)S(1)}, bf16[192,1536]{1,0:T(8,128)(2,1)}, u32[]{:S(2)}) copy-start(bf16[192,1536]{1,0:T(8,128)(2,1)} %refs_2_.1) | copy-start | bytes 1769476
  99.6 4.0 %copy-start.4 = (bf16[64,1024]{1,0:T(8,128)(2,1)S(1)}, bf16[64,1024]{1,0:T(8,128)(2,1)}, u32[]{:S(2)}) copy-start(bf16[64,1024]{1,0:T(8,128)(2,1)} %refs_3_.1) | copy-start | bytes 393220
